TPU v7x, 256 devices: a whole 4x4x8 slice. The times are simulated.
256 devices in a mesh: tm: 8 (over y, core), doc: 32 (over x, z).
Axes of the slice: x: 4, y: 4, z: 8, core: 2. Of those that a mesh axis runs over, the one named last changes fastest.
Arguments:
- beta_mean: float32 [16, 65536, 200], P('tm', 'doc'), may hold values from -9 to 230
- word_ids: int32 [8192, 128], P(('tm', 'doc')), may hold values from 0 to 65535, as said below
- word_counts: int32 [8192, 128], P(('tm', 'doc')), may hold values from 0 to 8
- doc_slice: int32 [8192], P(('tm', 'doc')), may hold values from 0 to 15, as said below
- dirichlet: float32 [200], replicated, may hold values from 0.05 to 0.5
- drift_var: float32 [200], replicated, may hold values from 0.002 to 0.5
- obs_var: float32 [200], replicated, may hold values from 0.05 to 1
Outputs:
- smoothed_mean: float32 [16, 65536, 200], P('tm', 'doc')
- doc_topics: float32 [8192, 200], P(('tm', 'doc'))
Inputs may be any that keep to these rules, and one draw needn't show every extreme that they name: `word_ids`: vocabulary range b holds the words b * 2048 to (b + 1) * 2048 - 1. Over the 4096 slots of each aligned block of 32 documents, at most 160 hold words of one range; in every block some range holds exactly 160, the same range for all blocks of the same 1024 documents. A word may fill several slots of a document. `doc_slice`: the documents of rows i * 1024 to (i + 1) * 1024 - 1 belong to slices i * 2 to (i + 1) * 2 - 1.
All inputs are finite; a program needn't handle non-finite values.
Results may differ from a plain program's by a relative error of at most 0.0034.
Values may be sent and summed in bfloat16 or wider, within the bound.
No kernel may reach another device: no remote copies, remote signals or barrier semaphores. Data moves between devices by JAX's collectives and lax.ppermute only.
A program may use at most 128 MiB of HBM per device.

v0:
```python
import jax
import jax.numpy as jnp
from jax import lax
from jax.sharding import PartitionSpec as P

E_ITERS = 4
pseudo_count = 0.1
prior_var = 1.0


def carried_in(value, axis, join, neutral):
    place = lax.axis_index(axis)
    gathered = jax.tree.map(
        lambda a, kind: lax.all_gather(a.astype(kind), axis), value, (jnp.bfloat16, jnp.bfloat16)
    )
    state = jax.tree.map(lambda a, e: jnp.zeros_like(a) + jnp.asarray(e, a.dtype), value, neutral)

    def one(hop, state):
        return join(
            state,
            jax.tree.map(
                lambda a, own: lax.dynamic_index_in_dim(a, hop, 0, False).astype(own.dtype),
                gathered,
                value,
            ),
        )

    return lax.fori_loop(0, place, one, state)


def entering(value, axis, join, neutral):
    count, mine = (lax.axis_size(axis), lax.axis_index(axis))
    pieces = jax.tree.map(lambda part: lax.all_gather(part, axis), value)
    pieces = jax.tree.map(lambda part: part[::-1], pieces)
    mine = count - 1 - mine
    total = jax.tree.map(
        lambda part, zero: jnp.full_like(part, 0) + jnp.asarray(zero, part.dtype), value, neutral
    )

    def hop(position, total):
        longer = join(total, jax.tree.map(lambda part: part[position], pieces))
        return jax.tree.map(lambda new, old: jnp.where(position < mine, new, old), longer, total)

    return lax.fori_loop(0, count - 1, hop, total)


def digamma_series(value):
    correction = jnp.zeros_like(value)
    for shift_step in range(6):
        correction = correction + 1.0 / (value + float(shift_step))
    shifted = value + 6.0
    inverse = 1.0 / shifted
    inverse_square = inverse * inverse
    series = inverse_square * (
        1.0 / 12.0 - inverse_square * (1.0 / 120.0 - inverse_square * (1.0 / 252.0))
    )
    return jnp.log(shifted) - 0.5 * inverse - series - correction


def expectation(tok_beta, tok_count, dirichlet):
    doc_gamma = dirichlet[None, :] + jnp.sum(tok_count, axis=1, keepdims=True) / dirichlet.shape[0]
    for iteration in range(E_ITERS):
        log_theta = digamma_series(doc_gamma) - digamma_series(
            jnp.sum(doc_gamma, axis=1, keepdims=True)
        )
        theta_exp = jnp.exp(log_theta)
        norm_tok = jnp.einsum(
            "dk,dnk->dn",
            theta_exp,
            tok_beta,
            precision=lax.Precision.HIGHEST,
            preferred_element_type=jnp.float32,
        )
        slot_ratio = tok_count / norm_tok
        doc_gamma = dirichlet[None, :] + theta_exp * jnp.einsum(
            "dn,dnk->dk",
            slot_ratio,
            tok_beta,
            precision=lax.Precision.HIGHEST,
            preferred_element_type=jnp.float32,
        )
    return (doc_gamma, theta_exp, slot_ratio)


def variances(drift_var, obs_var, length):

    def advance(filt_prev, placeholder):
        predicted = filt_prev + drift_var
        gain_now = predicted / (predicted + obs_var)
        filt_now = (1.0 - gain_now) * predicted
        return (filt_now, (gain_now, filt_now))

    initial = jnp.full(drift_var.shape, prior_var, jnp.float32)
    final_var, outputs = lax.scan(advance, initial, None, length=length)
    return outputs


def compose_maps(earlier, latter):
    return (latter[0] * earlier[0], latter[0][None, :] * earlier[1] + latter[1])


def per_device(beta_mean, word_ids, word_counts, doc_slice, dirichlet, drift_var, obs_var):
    slice_dev, vocab_shard, topics = beta_mean.shape
    doc_dev, token_width = word_ids.shape
    doc_peers = lax.axis_size("doc")
    time_peers = lax.axis_size("tm")
    time_index = lax.axis_index("tm")
    table_rows = slice_dev * vocab_shard
    vocab_top = lax.pmax(jnp.max(beta_mean, axis=1), "doc")
    vocab_total = lax.psum(jnp.sum(jnp.exp(beta_mean - vocab_top[:, None, :]), axis=1), "doc")
    log_norm = vocab_top + jnp.log(vocab_total)
    expected_beta = (
        jnp.exp(beta_mean - log_norm[:, None, :]).astype(jnp.bfloat16).reshape(table_rows, topics)
    )
    slot_count = doc_dev * token_width
    capacity = slot_count * 5 // (4 * doc_peers)
    flat_words = word_ids.reshape(slot_count)
    owners = flat_words // vocab_shard
    local_slice = doc_slice - time_index * slice_dev
    slot_row = jnp.repeat(local_slice, token_width) * vocab_shard + flat_words % vocab_shard
    slot_doc = jnp.repeat(jnp.arange(doc_dev, dtype=jnp.int32), token_width)
    request_code = slot_doc * table_rows + slot_row
    ordering = jnp.argsort(owners, stable=True)
    owners_sorted = owners[ordering]
    owner_load = jnp.sum(
        (owners[:, None] == jnp.arange(doc_peers, dtype=jnp.int32)[None, :]).astype(jnp.int32),
        axis=0,
    )
    owner_start = jnp.cumsum(owner_load) - owner_load
    place_sorted = (
        owners_sorted * capacity
        + jnp.arange(slot_count, dtype=jnp.int32)
        - owner_start[owners_sorted]
    )
    placement = jnp.zeros((slot_count,), jnp.int32).at[ordering].set(place_sorted)
    request = (
        jnp.full((doc_peers * capacity,), -1, jnp.int32)
        .at[placement]
        .set(request_code)
        .reshape(doc_peers, capacity)
    )
    received = lax.all_to_all(request, "doc", split_axis=0, concat_axis=0, tiled=True)
    rows_wanted = jnp.where(received >= 0, received % table_rows, 0)
    fetched = expected_beta[rows_wanted]
    replies = lax.all_to_all(fetched, "doc", split_axis=0, concat_axis=0, tiled=True)
    replies, received, fetched = (replies, received, fetched)
    tok_beta = replies.reshape(doc_peers * capacity, topics)[placement].reshape(
        doc_dev, token_width, topics
    )
    tok_count = word_counts.astype(jnp.float32)
    doc_gamma, theta_exp, slot_ratio = expectation(tok_beta, tok_count, dirichlet)
    slot_terms = (theta_exp[:, None, :] * slot_ratio[:, :, None]).reshape(slot_count, topics)
    outgoing = (
        jnp.zeros((doc_peers * capacity, topics), jnp.float32)
        .at[placement]
        .set(slot_terms)
        .reshape(doc_peers, capacity, topics)
    )
    arrived = lax.all_to_all(
        outgoing.astype(jnp.bfloat16), "doc", split_axis=0, concat_axis=0, tiled=True
    ).astype(outgoing.dtype)
    contrib = arrived * fetched
    target_row = jnp.where(received >= 0, received % table_rows, table_rows)
    word_stats = jax.ops.segment_sum(
        contrib.reshape(doc_peers * capacity, topics),
        target_row.reshape(doc_peers * capacity),
        num_segments=table_rows + 1,
    )
    word_stats = word_stats[:table_rows].reshape(slice_dev, vocab_shard, topics)
    total_slices = slice_dev * time_peers
    gain_all, var_all = variances(drift_var, obs_var, total_slices)
    first_slice = time_index * slice_dev
    gain_here = lax.dynamic_slice_in_dim(gain_all, first_slice, slice_dev, 0)
    var_here = lax.dynamic_slice_in_dim(var_all, first_slice, slice_dev, 0)
    slice_number = first_slice + jnp.arange(slice_dev, dtype=jnp.int32)
    smooth_gain = jnp.where(
        (slice_number == total_slices - 1)[:, None], 0.0, var_here / (var_here + drift_var[None, :])
    )
    pseudo = jnp.log(word_stats + pseudo_count)
    slope_now = jnp.ones((topics,), jnp.float32)
    offset = jnp.zeros((vocab_shard, topics), jnp.float32)
    slopes = []
    offsets = []
    for position in range(slice_dev):
        retained = 1.0 - gain_here[position]
        slope_now = retained * slope_now
        offset = retained[None, :] * offset + gain_here[position][None, :] * pseudo[position]
        slopes.append(slope_now)
        offsets.append(offset)
    identity = (jnp.ones((topics,), jnp.float32), jnp.zeros((vocab_shard, topics), jnp.float32))
    carried = carried_in((slope_now, offset), "tm", compose_maps, identity)
    filtered = [
        offsets[position] + slopes[position][None, :] * carried[1] for position in range(slice_dev)
    ]
    factor = jnp.ones((topics,), jnp.float32)
    constant = jnp.zeros((vocab_shard, topics), jnp.float32)
    factors = [None] * slice_dev
    constants = [None] * slice_dev
    for position in reversed(range(slice_dev)):
        weight = smooth_gain[position]
        factor = weight * factor
        constant = (1.0 - weight)[None, :] * filtered[position] + weight[None, :] * constant
        factors[position] = factor
        constants[position] = constant
    from_ahead = entering((factor, constant), "tm", compose_maps, identity)
    smoothed = jnp.stack(
        [
            constants[position] + factors[position][None, :] * from_ahead[1]
            for position in range(slice_dev)
        ]
    )
    return (smoothed, doc_gamma)


def solution(mesh):
    return jax.shard_map(
        per_device,
        mesh=mesh,
        in_specs=(
            P("tm", "doc", None),
            P(("tm", "doc"), None),
            P(("tm", "doc"), None),
            P(("tm", "doc")),
            P(),
            P(),
            P(),
        ),
        out_specs=(P("tm", "doc", None), P(("tm", "doc"), None)),
        check_vma=False,
    )
```

profile of v0, /device:TPU:1, one launch (start us, length us, event | category | flops | bytes accessed | tf_op | source)
XLA Modules:
  0.0 693.6 jit_solution(11381500754262118763)
XLA Ops:
  10.5 5.8 sort.17
  16.3 23.0 %gather_fusion = s32[4096]{0:T(1024)S(1)} fusion(s32[4096]{0:T(1024)S(1)} %get-tuple-element.318, s32[4096]{0:T(1024)S(1)} %get-tuple-element.319), kind=kCustom, calls=%fused_computation | custom fusion | bytes 49152 | tf_op jit(solution)/shard_map/gather | solution.py:124
  45.0 15.8 %select_subtract_fusion = s32[4096]{0:T(1024)S(1)} fusion(pred[4096]{0:T(1024)(128)(4,1)S(1)} %get-tuple-element.270, pred[4096]{0:T(1024)(128)(4,1)S(1)} %get-tuple-element.269, pred[4096]{0:T(1024)(128)(4,1)S(1)} %get-tuple-element.268, pred[4096]{0:T(1024)(128)(4,1)S(1)} %get-tuple-element.267, pred[4096]{0:T(1024)(128)(4,1)S(1)} %get-tuple-element.266, ...), kind=kLoop, calls=%fused_computation.139 | loop fusion | flops 114688 | bytes 151652 | tf_op jit(solution)/shard_map/sub | solution.py:131
  60.8 15.5 %scatter_custom_fusion = s32[4096]{0:T(1024)S(1)} fusion(s32[4096]{0:T(1024)S(1)} %get-tuple-element.320, s32[4096]{0:T(1024)S(1)} %select_subtract_fusion, s32[]{:T(128)} %constant.143.clone.1), kind=kCustom, calls=%fused_computation.157 | custom fusion | bytes 16388 | tf_op jit(solution)/shard_map/scatter | solution.py:135
  76.3 15.5 %scatter_custom_fusion.1 = s32[5120]{0:T(1024)S(1)} fusion(s32[4096]{0:T(1024)S(1)} %get-tuple-element.316, s32[4096]{0:T(1024)S(1)} %get-tuple-element.317, s32[]{:T(128)} %constant.145.clone.1), kind=kCustom, calls=%fused_computation.150 | custom fusion | bytes 20484 | tf_op jit(solution)/shard_map/scatter | solution.py:139
  92.6 11.9 %all-to-all-start = ((s32[32,1,160]{2,1,0:T(1,128)}), s32[32,1,160]{2,1,0:T(1,128)S(1)}, u32[]{:S(2)}, u32[]{:S(2)}) async-start(s32[32,1,160]{2,1,0:T(1,128)} %all_to_all.16), calls=%async_computation | async-start | bytes 65536 | tf_op jit(solution)/shard_map/all_to_all | solution.py:142
  104.7 60.5 %pmax.7 = f32[2,200]{1,0:T(2,128)S(1)} all-reduce(f32[2,200]{1,0:T(2,128)S(1)} %reduce_max.9), channel_id=1, replica_groups=mesh['tm'=8,'doc'=32] {'doc'}, use_global_device_ids=true, to_apply=%region_10.11 | all-reduce | flops 400 | bytes 3200 | tf_op jit(solution)/shard_map/pmax | solution.py:109
  165.8 55.7 %psum.7 = f32[2,200]{1,0:T(2,128)S(1)} all-reduce(f32[2,200]{1,0:T(2,128)S(1)} %exponential_reduce_fusion), channel_id=1, replica_groups=mesh['tm'=8,'doc'=32] {'doc'}, use_global_device_ids=true, to_apply=%region_12.13 | all-reduce | flops 400 | bytes 3200 | tf_op jit(solution)/shard_map/psum | solution.py:110
  226.3 21.1 %gather_fusion.1 = bf16[5120,200]{1,0:T(8,128)(2,1)} fusion(bf16[4096,200]{1,0:T(8,128)(2,1)S(1)} %bitcast.213, s32[5120]{0:T(1024)S(1)} %broadcast_clamp_fusion), kind=kCustom, calls=%fused_computation.1 | custom fusion | bytes 4116480 | tf_op jit(solution)/shard_map/gather | solution.py:144
  252.3 32.8 %all-to-all-done.1 = bf16[32,160,200]{2,1,0:T(8,128)(2,1)S(1)} async-done(((bf16[32,160,200]{2,1,0:T(8,128)(2,1)}), bf16[32,160,200]{2,1,0:T(8,128)(2,1)S(1)}, u32[]{:S(2)}, u32[]{:S(2)}) %all-to-all-start.1) | async-done | bytes 2048032 | tf_op jit(solution)/shard_map/all_to_all | solution.py:145
  286.7 15.1 %gather_fusion.2 = bf16[4096,200]{1,0:T(8,128)(2,1)S(1)} fusion(bf16[5120,200]{1,0:T(8,128)(2,1)} %bitcast.222, s32[4096]{0:T(1024)S(1)} %get-tuple-element.315), kind=kCustom, calls=%fused_computation.2 | custom fusion | bytes 3293184 | tf_op jit(solution)/shard_map/gather | solution.py:147
  315.1 20.4 %scatter_custom_fusion.2 = f32[5120,200]{1,0:T(8,128)} fusion(s32[4096]{0:T(1024)S(1)} %get-tuple-element.316, f32[4096,200]{1,0:T(8,128)} %bitcast_multiply_fusion, f32[]{:T(128)} %constant.142.clone.1), kind=kCustom, calls=%fused_computation.23 | custom fusion | bytes 4096512 | tf_op jit(solution)/shard_map/scatter | solution.py:156
  339.8 6.6 all-to-all-start.2
  349.2 30.7 %all-to-all-done.2 = bf16[32,160,200]{2,1,0:T(8,128)(2,1)} async-done(((bf16[32,160,200]{2,1,0:T(8,128)(2,1)}), bf16[32,160,200]{2,1,0:T(8,128)(2,1)}, u32[]{:S(2)}, u32[]{:S(2)}) %all-to-all-start.2) | async-done | bytes 2048032 | tf_op jit(solution)/shard_map/all_to_all | solution.py:159
  379.9 5.7 convert_multiply_fusion
  385.6 33.4 %scatter_custom_fusion.3 = f32[4097,200]{1,0:T(8,128)} fusion(s32[5120]{0:T(1024)S(1)} %bitcast.253, f32[5120,200]{1,0:T(8,128)} %bitcast.227, f32[]{:T(128)} %constant.142.clone.1), kind=kCustom, calls=%fused_computation.25 | custom fusion | flops 1024000 | bytes 3278112 | tf_op jit(solution)/shard_map/scatter-add | solution.py:164
  425.5 42.1 %all-gather.1 = bf16[8,1,200]{2,1,0:T(2,128)(2,1)S(1)} all-gather(bf16[1,1,200]{2,1,0:T(2,128)(2,1)S(1)} %get-tuple-element.311), channel_id=1, replica_groups=mesh['tm'=8,'doc'=32] {'tm'}, dimensions={0}, use_global_device_ids=true | all-gather | bytes 3600 | tf_op jit(solution)/shard_map/all_gather | solution.py:14
  467.6 29.5 %all-gather.6.cloned.1.call-done = bf16[8,2048,200]{1,2,0:T(8,128)(2,1)} async-done(((bf16[1,2048,200]{1,2,0:T(8,128)(2,1)}), bf16[8,2048,200]{1,2,0:T(8,128)(2,1)}) %all-gather.6.cloned.1.call-update) | async-done | bytes 6553616 | tf_op jit(solution)/shard_map/all_gather | solution.py:14
  498.6 6.7 while.41
  510.5 46.9 %all-gather.2 = f32[8,1,200]{2,1,0:T(1,128)S(1)} all-gather(f32[1,1,200]{2,1,0:T(1,128)S(1)} %bitcast.257), channel_id=1, replica_groups=mesh['tm'=8,'doc'=32] {'tm'}, dimensions={0}, use_global_device_ids=true | all-gather | bytes 7200 | tf_op jit(solution)/shard_map/all_gather | solution.py:33
  558.9 78.5 %all-gather.8.cloned.1.call-done = f32[16384,200]{1,0:T(8,128)} async-done(((f32[2048,200]{1,0:T(8,128)}), f32[16384,200]{1,0:T(8,128)}) %all-gather.8.cloned.1.call-update) | async-done | bytes 13107216 | tf_op jit(solution)/shard_map/all_gather | solution.py:33
  637.5 11.3 %rev.7 = f32[8,2048,200]{2,1,0:T(8,128)} reverse(f32[8,2048,200]{2,1,0:T(8,128)} %bitcast.225), dimensions={0} | reverse | bytes 26214400 | tf_op jit(solution)/shard_map/rev | solution.py:34
  648.7 26.2 %while.43 = (s32[]{:T(128)}, f32[2048,200]{1,0:T(8,128)}, s32[]{:T(128)}, f32[8,200]{1,0:T(8,128)S(1)}, f32[8,2048,200]{2,1,0:T(8,128)}, /*index=5*/s32[]{:T(128)}, s32[]{:T(128)}) while((s32[]{:T(128)}, f32[2048,200]{1,0:T(8,128)}, s32[]{:T(128)}, f32[8,200]{1,0:T(8,128)S(1)}, f32[8,2048,200]{2,1,0:T(8,128)}, ...), condition=%wide.region_21.22_spmd.clone, body=%wide.region_20.21_spmd.clone.sunk | while | flops 1638404 | bytes 4917713 | solution.py:44
  681.5 5.2 copy.35
  (164 shorter events, 97.6 us)
Async XLA Ops:
  16.3 88.2 %copy-start.3 = (f32[2,2048,200]{1,2,0:T(8,128)S(1)}, f32[2,2048,200]{1,2,0:T(8,128)}, u32[]{:S(2)}) copy-start(f32[2,2048,200]{1,2,0:T(8,128)} %param.13) | copy-start | bytes 9830404
  92.6 133.4 %all-to-all-start = ((s32[32,1,160]{2,1,0:T(1,128)}), s32[32,1,160]{2,1,0:T(1,128)S(1)}, u32[]{:S(2)}, u32[]{:S(2)}) async-start(s32[32,1,160]{2,1,0:T(1,128)} %all_to_all.16), calls=%async_computation | async-start | bytes 65536 | tf_op jit(solution)/shard_map/all_to_all | solution.py:142
  247.4 4.4 copy-start.4
  247.4 4.6 copy-start.5
  247.4 37.7 %all-to-all-start.1 = ((bf16[32,160,200]{2,1,0:T(8,128)(2,1)}), bf16[32,160,200]{2,1,0:T(8,128)(2,1)S(1)}, u32[]{:S(2)}, u32[]{:S(2)}) async-start(bf16[32,160,200]{2,1,0:T(8,128)(2,1)} %bitcast.223), calls=%async_computation.1 | async-start | bytes 5242880 | tf_op jit(solution)/shard_map/all_to_all | solution.py:145
  285.2 1.5 copy-start
  339.8 6.9 copy-start.6
  339.8 6.9 copy-start.7
  339.8 40.1 %all-to-all-start.2 = ((bf16[32,160,200]{2,1,0:T(8,128)(2,1)}), bf16[32,160,200]{2,1,0:T(8,128)(2,1)}, u32[]{:S(2)}, u32[]{:S(2)}) async-start(bf16[32,160,200]{2,1,0:T(8,128)(2,1)} %bitcast.226), calls=%async_computation.2 | async-start | bytes 5242880 | tf_op jit(solution)/shard_map/all_to_all | solution.py:159
  346.4 150.8 %all-gather.6.cloned.1.call-start = ((), (), s32[]{:S(2)}) async-start(), calls=%async_computation.3 | async-start | bytes 7372800 | tf_op jit(solution)/shard_map/all_gather | solution.py:14
  421.7 2.0 copy-start.2
  425.4 212.0 %all-gather.8.cloned.1.call-start = ((), (), s32[]{:S(2)}) async-start(), calls=%async_computation.4 | async-start | bytes 18874368 | tf_op jit(solution)/shard_map/all_gather | solution.py:33
  648.7 26.2 %copy-start.1 = (f32[2048,200]{1,0:T(8,128)S(1)}, f32[2048,200]{1,0:T(8,128)}, u32[]{:S(2)}) copy-start(f32[2048,200]{1,0:T(8,128)} %get-tuple-element.177) | copy-start | bytes 4915204
Sparse Core Ops, SparseCore 0:
  425.6 71.5 all-gather.5
  510.6 126.8 all-gather.7
where the time goes:
time: 695 us; the launch traced here: 694 us
  blocking collectives  205 us (29%)
  waiting for transfers between devices  172 us (25%)
  local copies, waits for them, and re-layouts  144 us (21%)
  other arithmetic  124 us (18%)
  starting transfers between devices  23.1 us (3%)
  between operations  14.4 us (2%)
  matrix products  10.6 us (2%)
    all_gather x1, waiting for transfers between devices, entering(): pieces = jax.tree.map(lambda part: lax.all_gather(part, axis), value)  78.5 us
    pmax x1, blocking collectives, per_device(): vocab_top = lax.pmax(jnp.max(beta_mean, axis=1), 'doc')  60.5 us
    psum x1, blocking collectives, per_device(): lax.psum(jnp.sum(jnp.exp(beta_mean - vocab_top[:, None, :]), axis=1), 'doc')  55.7 us
    all_gather x1, blocking collectives, entering(): pieces = jax.tree.map(lambda part: lax.all_gather(part, axis), value)  46.9 us
    all_gather x1, blocking collectives, carried_in(): lax.all_gather(a.astype(kind), axis)  42.1 us
    scatter-add x1, other arithmetic, per_device(): jax.ops.segment_sum(contrib.reshape(doc_peers * capacity, topics), target...  33.4 us
    all_to_all x1, waiting for transfers between devices, per_device(): lax.all_to_all(fetched, 'doc', split_axis=0, concat_axis=0, tiled=True)  32.8 us
    all_to_all x1, waiting for transfers between devices, per_device(): lax.all_to_all(outgoing.astype(jnp.bfloat16), 'doc', split_axis=0, concat...  30.7 us
  transfers between devices with their start and end apart: 5, of which 4 were waited for; matrix products, arithmetic and copies ran while one was open for 1% of the time, Pallas kernels for 0%

commit v1 on v0

--- a/solution.py
+++ b/solution.py
@@ -100,6 +100,10 @@
 
 
 def per_device(beta_mean, word_ids, word_counts, doc_slice, dirichlet, drift_var, obs_var):
+
+    def _pass_grid(shard_in):
+        return jnp.sum(lax.all_gather(shard_in, "doc"), axis=0)
+
     slice_dev, vocab_shard, topics = beta_mean.shape
     doc_dev, token_width = word_ids.shape
     doc_peers = lax.axis_size("doc")
@@ -107,7 +111,7 @@
     time_index = lax.axis_index("tm")
     table_rows = slice_dev * vocab_shard
     vocab_top = lax.pmax(jnp.max(beta_mean, axis=1), "doc")
-    vocab_total = lax.psum(jnp.sum(jnp.exp(beta_mean - vocab_top[:, None, :]), axis=1), "doc")
+    vocab_total = _pass_grid(jnp.sum(jnp.exp(beta_mean - vocab_top[:, None, :]), axis=1))
     log_norm = vocab_top + jnp.log(vocab_total)
     expected_beta = (
         jnp.exp(beta_mean - log_norm[:, None, :]).astype(jnp.bfloat16).reshape(table_rows, topics)

time: 695 us -> 674 us (0.970)
  blocking collectives: 205 us -> 182 us
    psum x1 -> x0, blocking collectives: 55.7 us -> none  [per_device(): lax.psum(jnp.sum(jnp.exp(beta_mean - vocab_top[:, None, :]), axis=1), 'doc')]
    all_gather x0 -> x1, blocking collectives: none -> 33.4 us  [_pass_grid(): return jnp.sum(lax.all_gather(shard_in, 'doc'), axis=0)]
where the time goes in v1:
time: 674 us; the launch traced here: 672 us
  blocking collectives  182 us (27%)
  waiting for transfers between devices  171 us (25%)
  local copies, waits for them, and re-layouts  144 us (21%)
  other arithmetic  124 us (18%)
  starting transfers between devices  25.9 us (4%)
  between operations  14.4 us (2%)
  matrix products  10.6 us (2%)
    all_gather x1, waiting for transfers between devices, entering(): pieces = jax.tree.map(lambda part: lax.all_gather(part, axis), value)  78.5 us
    pmax x1, blocking collectives, per_device(): vocab_top = lax.pmax(jnp.max(beta_mean, axis=1), 'doc')  60.5 us
    all_gather x1, blocking collectives, entering(): pieces = jax.tree.map(lambda part: lax.all_gather(part, axis), value)  46.9 us
    all_gather x1, blocking collectives, carried_in(): lax.all_gather(a.astype(kind), axis)  41.2 us
    all_gather x1, blocking collectives, _pass_grid(): return jnp.sum(lax.all_gather(shard_in, 'doc'), axis=0)  33.4 us
    scatter-add x1, other arithmetic, per_device(): jax.ops.segment_sum(contrib.reshape(doc_peers * capacity, topics), target...  33.4 us
    all_to_all x1, waiting for transfers between devices, per_device(): lax.all_to_all(fetched, 'doc', split_axis=0, concat_axis=0, tiled=True)  33.1 us
    all_to_all x1, waiting for transfers between devices, per_device(): lax.all_to_all(outgoing.astype(jnp.bfloat16), 'doc', split_axis=0, concat...  30.9 us
  transfers between devices with their start and end apart: 5, of which 4 were waited for; matrix products, arithmetic and copies ran while one was open for 1% of the time, Pallas kernels for 0%

profile of v1, /device:TPU:1, one launch (start us, length us, event | category | flops | bytes accessed | tf_op | source)
XLA Modules:
  0.0 672.2 jit_solution(7198192125145790724)
XLA Ops:
  10.5 5.8 sort.17
  16.3 23.0 %gather_fusion = s32[4096]{0:T(1024)S(1)} fusion(s32[4096]{0:T(1024)S(1)} %get-tuple-element.318, s32[4096]{0:T(1024)S(1)} %get-tuple-element.319), kind=kCustom, calls=%fused_computation | custom fusion | bytes 49152 | tf_op jit(solution)/shard_map/gather | solution.py:128
  45.0 15.8 %select_subtract_fusion = s32[4096]{0:T(1024)S(1)} fusion(pred[4096]{0:T(1024)(128)(4,1)S(1)} %get-tuple-element.270, pred[4096]{0:T(1024)(128)(4,1)S(1)} %get-tuple-element.269, pred[4096]{0:T(1024)(128)(4,1)S(1)} %get-tuple-element.268, pred[4096]{0:T(1024)(128)(4,1)S(1)} %get-tuple-element.267, pred[4096]{0:T(1024)(128)(4,1)S(1)} %get-tuple-element.266, ...), kind=kLoop, calls=%fused_computation.139 | loop fusion | flops 114688 | bytes 151652 | tf_op jit(solution)/shard_map/sub | solution.py:135
  60.8 15.5 %scatter_custom_fusion = s32[4096]{0:T(1024)S(1)} fusion(s32[4096]{0:T(1024)S(1)} %get-tuple-element.320, s32[4096]{0:T(1024)S(1)} %select_subtract_fusion, s32[]{:T(128)} %constant.143.clone.1), kind=kCustom, calls=%fused_computation.157 | custom fusion | bytes 16388 | tf_op jit(solution)/shard_map/scatter | solution.py:139
  76.3 15.5 %scatter_custom_fusion.1 = s32[5120]{0:T(1024)S(1)} fusion(s32[4096]{0:T(1024)S(1)} %get-tuple-element.316, s32[4096]{0:T(1024)S(1)} %get-tuple-element.317, s32[]{:T(128)} %constant.145.clone.1), kind=kCustom, calls=%fused_computation.150 | custom fusion | bytes 20484 | tf_op jit(solution)/shard_map/scatter | solution.py:143
  92.6 11.9 %all-to-all-start = ((s32[32,1,160]{2,1,0:T(1,128)}), s32[32,1,160]{2,1,0:T(1,128)S(1)}, u32[]{:S(2)}, u32[]{:S(2)}) async-start(s32[32,1,160]{2,1,0:T(1,128)} %all_to_all.16), calls=%async_computation | async-start | bytes 65536 | tf_op jit(solution)/shard_map/all_to_all | solution.py:146
  104.7 60.5 %pmax.7 = f32[2,200]{1,0:T(2,128)S(1)} all-reduce(f32[2,200]{1,0:T(2,128)S(1)} %reduce_max.9), channel_id=1, replica_groups=mesh['tm'=8,'doc'=32] {'doc'}, use_global_device_ids=true, to_apply=%region_10.11 | all-reduce | flops 400 | bytes 3200 | tf_op jit(solution)/shard_map/pmax | solution.py:113
  165.8 33.4 %all-gather.2 = f32[32,2,200]{2,1,0:T(2,128)S(1)} all-gather(f32[1,2,200]{2,1,0:T(2,128)S(1)} %bitcast.268), channel_id=2, replica_groups=mesh['tm'=8,'doc'=32] {'doc'}, dimensions={0}, use_global_device_ids=true | all-gather | bytes 52800 | tf_op jit(solution)/shard_map/all_gather | solution.py:105
  204.1 21.1 %gather_fusion.1 = bf16[5120,200]{1,0:T(8,128)(2,1)} fusion(bf16[4096,200]{1,0:T(8,128)(2,1)S(1)} %bitcast.214, s32[5120]{0:T(1024)S(1)} %broadcast_clamp_fusion), kind=kCustom, calls=%fused_computation.1 | custom fusion | bytes 4116480 | tf_op jit(solution)/shard_map/gather | solution.py:148
  225.2 6.0 all-to-all-start.1
  231.7 33.1 %all-to-all-done.1 = bf16[32,160,200]{2,1,0:T(8,128)(2,1)S(1)} async-done(((bf16[32,160,200]{2,1,0:T(8,128)(2,1)}), bf16[32,160,200]{2,1,0:T(8,128)(2,1)S(1)}, u32[]{:S(2)}, u32[]{:S(2)}) %all-to-all-start.1) | async-done | bytes 2048032 | tf_op jit(solution)/shard_map/all_to_all | solution.py:149
  266.3 15.1 %gather_fusion.2 = bf16[4096,200]{1,0:T(8,128)(2,1)S(1)} fusion(bf16[5120,200]{1,0:T(8,128)(2,1)} %bitcast.223, s32[4096]{0:T(1024)S(1)} %get-tuple-element.315), kind=kCustom, calls=%fused_computation.2 | custom fusion | bytes 3293184 | tf_op jit(solution)/shard_map/gather | solution.py:151
  294.7 20.4 %scatter_custom_fusion.2 = f32[5120,200]{1,0:T(8,128)} fusion(s32[4096]{0:T(1024)S(1)} %get-tuple-element.316, f32[4096,200]{1,0:T(8,128)} %bitcast_multiply_fusion, f32[]{:T(128)} %constant.142.clone.1), kind=kCustom, calls=%fused_computation.23 | custom fusion | bytes 4096512 | tf_op jit(solution)/shard_map/scatter | solution.py:160
  319.4 7.7 %all-to-all-start.2 = ((bf16[32,160,200]{2,1,0:T(8,128)(2,1)}), bf16[32,160,200]{2,1,0:T(8,128)(2,1)}, u32[]{:S(2)}, u32[]{:S(2)}) async-start(bf16[32,160,200]{2,1,0:T(8,128)(2,1)} %bitcast.227), calls=%async_computation.2 | async-start | bytes 5242880 | tf_op jit(solution)/shard_map/all_to_all | solution.py:163
  329.9 30.9 %all-to-all-done.2 = bf16[32,160,200]{2,1,0:T(8,128)(2,1)} async-done(((bf16[32,160,200]{2,1,0:T(8,128)(2,1)}), bf16[32,160,200]{2,1,0:T(8,128)(2,1)}, u32[]{:S(2)}, u32[]{:S(2)}) %all-to-all-start.2) | async-done | bytes 2048032 | tf_op jit(solution)/shard_map/all_to_all | solution.py:163
  360.8 5.7 convert_multiply_fusion
  366.5 33.4 %scatter_custom_fusion.3 = f32[4097,200]{1,0:T(8,128)} fusion(s32[5120]{0:T(1024)S(1)} %bitcast.254, f32[5120,200]{1,0:T(8,128)} %bitcast.228, f32[]{:T(128)} %constant.142.clone.1), kind=kCustom, calls=%fused_computation.25 | custom fusion | flops 1024000 | bytes 3278112 | tf_op jit(solution)/shard_map/scatter-add | solution.py:168
  406.4 41.2 %all-gather.3 = bf16[8,1,200]{2,1,0:T(2,128)(2,1)S(1)} all-gather(bf16[1,1,200]{2,1,0:T(2,128)(2,1)S(1)} %get-tuple-element.311), channel_id=1, replica_groups=mesh['tm'=8,'doc'=32] {'tm'}, dimensions={0}, use_global_device_ids=true | all-gather | bytes 3600 | tf_op jit(solution)/shard_map/all_gather | solution.py:14
  447.6 28.1 %all-gather.8.cloned.1.call-done = bf16[8,2048,200]{1,2,0:T(8,128)(2,1)} async-done(((bf16[1,2048,200]{1,2,0:T(8,128)(2,1)}), bf16[8,2048,200]{1,2,0:T(8,128)(2,1)}) %all-gather.8.cloned.1.call-update) | async-done | bytes 6553616 | tf_op jit(solution)/shard_map/all_gather | solution.py:14
  477.2 6.7 while.41
  489.0 46.9 %all-gather.4 = f32[8,1,200]{2,1,0:T(1,128)S(1)} all-gather(f32[1,1,200]{2,1,0:T(1,128)S(1)} %bitcast.258), channel_id=1, replica_groups=mesh['tm'=8,'doc'=32] {'tm'}, dimensions={0}, use_global_device_ids=true | all-gather | bytes 7200 | tf_op jit(solution)/shard_map/all_gather | solution.py:33
  537.5 78.5 %all-gather.10.cloned.1.call-done = f32[16384,200]{1,0:T(8,128)} async-done(((f32[2048,200]{1,0:T(8,128)}), f32[16384,200]{1,0:T(8,128)}) %all-gather.10.cloned.1.call-update) | async-done | bytes 13107216 | tf_op jit(solution)/shard_map/all_gather | solution.py:33
  616.0 11.3 %rev.7 = f32[8,2048,200]{2,1,0:T(8,128)} reverse(f32[8,2048,200]{2,1,0:T(8,128)} %bitcast.226), dimensions={0} | reverse | bytes 26214400 | tf_op jit(solution)/shard_map/rev | solution.py:34
  627.3 26.2 %while.43 = (s32[]{:T(128)}, f32[2048,200]{1,0:T(8,128)}, s32[]{:T(128)}, f32[8,200]{1,0:T(8,128)S(1)}, f32[8,2048,200]{2,1,0:T(8,128)}, /*index=5*/s32[]{:T(128)}, s32[]{:T(128)}) while((s32[]{:T(128)}, f32[2048,200]{1,0:T(8,128)}, s32[]{:T(128)}, f32[8,200]{1,0:T(8,128)S(1)}, f32[8,2048,200]{2,1,0:T(8,128)}, ...), condition=%wide.region_21.22_spmd.clone, body=%wide.region_20.21_spmd.clone.sunk | while | flops 1638404 | bytes 4917713 | solution.py:44
  (165 shorter events, 98.5 us)
Async XLA Ops:
  16.3 88.2 %copy-start.3 = (f32[2,2048,200]{1,2,0:T(8,128)S(1)}, f32[2,2048,200]{1,2,0:T(8,128)}, u32[]{:S(2)}) copy-start(f32[2,2048,200]{1,2,0:T(8,128)} %param.13) | copy-start | bytes 9830404
  92.6 111.2 %all-to-all-start = ((s32[32,1,160]{2,1,0:T(1,128)}), s32[32,1,160]{2,1,0:T(1,128)S(1)}, u32[]{:S(2)}, u32[]{:S(2)}) async-start(s32[32,1,160]{2,1,0:T(1,128)} %all_to_all.16), calls=%async_computation | async-start | bytes 65536 | tf_op jit(solution)/shard_map/all_to_all | solution.py:146
  225.2 6.1 copy-start.4
  225.2 6.2 copy-start.5
  225.2 39.6 %all-to-all-start.1 = ((bf16[32,160,200]{2,1,0:T(8,128)(2,1)}), bf16[32,160,200]{2,1,0:T(8,128)(2,1)S(1)}, u32[]{:S(2)}, u32[]{:S(2)}) async-start(bf16[32,160,200]{2,1,0:T(8,128)(2,1)} %bitcast.224), calls=%async_computation.1 | async-start | bytes 5242880 | tf_op jit(solution)/shard_map/all_to_all | solution.py:149
  264.8 1.5 copy-start
  319.4 8.0 %copy-start.6 = (f32[200]{0:T(256)S(1)}, f32[200]{0:T(256)}, u32[]{:S(2)}) copy-start(f32[200]{0:T(256)} %param.18) | copy-start | bytes 2404
  319.4 8.0 %copy-start.7 = (f32[200]{0:T(256)S(1)}, f32[200]{0:T(256)}, u32[]{:S(2)}) copy-start(f32[200]{0:T(256)} %param.19) | copy-start | bytes 2404
  319.4 41.4 %all-to-all-start.2 = ((bf16[32,160,200]{2,1,0:T(8,128)(2,1)}), bf16[32,160,200]{2,1,0:T(8,128)(2,1)}, u32[]{:S(2)}, u32[]{:S(2)}) async-start(bf16[32,160,200]{2,1,0:T(8,128)(2,1)} %bitcast.227), calls=%async_computation.2 | async-start | bytes 5242880 | tf_op jit(solution)/shard_map/all_to_all | solution.py:163
  327.1 148.6 %all-gather.8.cloned.1.call-start = ((), (), s32[]{:S(2)}) async-start(), calls=%async_computation.3 | async-start | bytes 7372800 | tf_op jit(solution)/shard_map/all_gather | solution.py:14
  402.6 2.0 copy-start.2
  406.3 209.7 %all-gather.10.cloned.1.call-start = ((), (), s32[]{:S(2)}) async-start(), calls=%async_computation.4 | async-start | bytes 18874368 | tf_op jit(solution)/shard_map/all_gather | solution.py:33
  627.3 26.2 %copy-start.1 = (f32[2048,200]{1,0:T(8,128)S(1)}, f32[2048,200]{1,0:T(8,128)}, u32[]{:S(2)}) copy-start(f32[2048,200]{1,0:T(8,128)} %get-tuple-element.177) | copy-start | bytes 4915204
Sparse Core Ops, SparseCore 0:
  406.5 69.2 all-gather.7
  489.1 126.8 all-gather.9
